TPU v7x, 32 devices: a whole 2x2x4 slice. The times are simulated.
32 devices in a mesh: dp: 8 (over y, x, core), tensor: 4 (over z).
Axes of the slice: x: 2, y: 2, z: 4, core: 2. Of those that a mesh axis runs over, the one named last changes fastest.
Arguments:
- hidden: bfloat16 [8192, 2048], P(('dp', 'tensor')), may hold values from -6 to 6
- seq_lengths: int32 [8], P('dp'), may hold values from 1 to 1024, 6144 in all
- attn_norm_gain: float32 [2048], P(('dp', 'tensor')), may hold values from 0.5 to 1.5
- attn_norm_bias: float32 [2048], P(('dp', 'tensor')), may hold values from -1.25 to 1.25
- query_weight: bfloat16 [2048, 2048], P('dp', 'tensor'), may hold values from -0.1875 to 0.1875
- key_weight: bfloat16 [2048, 2048], P('dp', 'tensor'), may hold values from -0.1875 to 0.1875
- value_weight: bfloat16 [2048, 2048], P('dp', 'tensor'), may hold values from -0.125 to 0.125
- query_bias: bfloat16 [16, 128], P('tensor', 'dp'), may hold values from -1.25 to 1.25
- value_bias: bfloat16 [16, 128], P('tensor', 'dp'), may hold values from -1.25 to 1.25
- output_weight: bfloat16 [2048, 2048], P('tensor', 'dp'), may hold values from -0.375 to 0.375
- output_bias: float32 [2048], P(('dp', 'tensor')), may hold values from -1.25 to 1.25
- mlp_norm_gain: float32 [2048], P(('dp', 'tensor')), may hold values from 0.5 to 1.5
- mlp_norm_bias: float32 [2048], P(('dp', 'tensor')), may hold values from -1.25 to 1.25
- up_weight: bfloat16 [2048, 8192], P('dp', 'tensor'), may hold values from -0.125 to 0.125
- up_bias: bfloat16 [64, 128], P('tensor', 'dp'), may hold values from -1.25 to 1.25
- down_weight: bfloat16 [8192, 2048], P('tensor', 'dp'), may hold values from -0.09375 to 0.09375
- down_bias: float32 [2048], P(('dp', 'tensor')), may hold values from -1.25 to 1.25
- out_grad: bfloat16 [8192, 2048], P(('dp', 'tensor')), may hold values from -6 to 6
Outputs:
- layer_out: bfloat16 [8192, 2048], P(('dp', 'tensor'))
- hidden_grad: float32 [8192, 2048], P(('dp', 'tensor'))
- attn_norm_gain_grad: float32 [2048], P(('dp', 'tensor'))
- attn_norm_bias_grad: float32 [2048], P(('dp', 'tensor'))
- query_weight_grad: float32 [2048, 2048], P('dp', 'tensor')
- key_weight_grad: float32 [2048, 2048], P('dp', 'tensor')
- value_weight_grad: float32 [2048, 2048], P('dp', 'tensor')
- query_bias_grad: float32 [16, 128], P('tensor', 'dp')
- value_bias_grad: float32 [16, 128], P('tensor', 'dp')
- output_weight_grad: float32 [2048, 2048], P('tensor', 'dp')
- output_bias_grad: float32 [2048], P(('dp', 'tensor'))
- mlp_norm_gain_grad: float32 [2048], P(('dp', 'tensor'))
- mlp_norm_bias_grad: float32 [2048], P(('dp', 'tensor'))
- up_weight_grad: float32 [2048, 8192], P('dp', 'tensor')
- up_bias_grad: float32 [64, 128], P('tensor', 'dp')
- down_weight_grad: float32 [8192, 2048], P('tensor', 'dp')
- down_bias_grad: float32 [2048], P(('dp', 'tensor'))
Inputs may be any that keep to these rules, and one draw needn't show every extreme that they name: `seq_lengths`: the number of tokens at the start of each sequence's 1024 slots; the rest are padding.
All inputs are finite; a program needn't handle non-finite values. No bound on the sum of `seq_lengths` on one device may be relied on, other than what follows from the above.
Results may differ from a plain program's by a relative error of at most 0.017.
Values may be sent and summed in bfloat16 or wider, within the bound.
A program may use at most 152 MiB of HBM per device.

v0:
```python
import math

import jax
import jax.numpy as jnp
from jax import lax
from jax.sharding import PartitionSpec as P

H = 16
HD = 128


EPSILON = 1e-05
GELU_COEF = math.sqrt(2.0 / math.pi)
NEGATIVE = -1e30


def norm_forward(values, norm_gain, norm_bias):
    center = values - jnp.mean(values, axis=-1, keepdims=True)
    inverse = lax.rsqrt(jnp.mean(center * center, axis=-1, keepdims=True) + EPSILON)
    normed = center * inverse
    return (normed * norm_gain + norm_bias, normed, inverse)


def norm_backward(upstream, normed, inverse, norm_gain):
    scaled = upstream * norm_gain
    inner_term = (
        scaled
        - jnp.mean(scaled, axis=-1, keepdims=True)
        - normed * jnp.mean(scaled * normed, axis=-1, keepdims=True)
    )
    return (inner_term * inverse, jnp.sum(upstream * normed, axis=0), jnp.sum(upstream, axis=0))


def gelu_pair(values):
    tanh_val = jnp.tanh(GELU_COEF * (values + 0.044715 * values * values * values))
    act_value = 0.5 * values * (1.0 + tanh_val)
    act_slope = 0.5 * (1.0 + tanh_val) + 0.5 * values * (1.0 - tanh_val * tanh_val) * GELU_COEF * (
        1.0 + 3.0 * 0.044715 * values * values
    )
    return (act_value, act_slope)


def dot_rows(left_mat, right_mat):
    return lax.dot_general(
        left_mat, right_mat, (((0,), (0,)), ((), ())), preferred_element_type=jnp.float32
    )


def dot_trans(left_mat, right_mat):
    return lax.dot_general(
        left_mat, right_mat, (((1,), (1,)), ((), ())), preferred_element_type=jnp.float32
    )


def block_layout(key_rows):
    block_rows = min(512, key_rows)
    return (block_rows, key_rows // block_rows)


def block_scores(query_block, keys_all, first_row, slopes, seq_len):
    block_rows = query_block.shape[0]
    key_rows = keys_all.shape[0]
    scale = 1.0 / math.sqrt(keys_all.shape[2])
    scores = (
        jnp.einsum("qhd,khd->hqk", query_block, keys_all, preferred_element_type=jnp.float32)
        * scale
    )
    query_pos = first_row + lax.iota(jnp.int32, block_rows)
    key_pos = lax.iota(jnp.int32, key_rows)
    distance = (query_pos[:, None] - key_pos[None, :]).astype(jnp.float32)
    scores = scores - slopes[:, None, None] * distance
    allowed = (key_pos[None, :] <= query_pos[:, None]) & (key_pos[None, :] < seq_len)
    return jnp.where(allowed[None], scores, NEGATIVE)


def attend_forward(queries, keys_all, values_all, slopes, seq_len):
    key_rows, head_count, head_dim = queries.shape
    block_rows, block_count = block_layout(key_rows)
    blocks = queries.reshape(block_count, block_rows, head_count, head_dim)
    starts = lax.iota(jnp.int32, block_count) * block_rows

    def one_block(inputs):
        query_block, first_row = inputs
        scores = block_scores(query_block, keys_all, first_row, slopes, seq_len)
        row_max = jnp.max(scores, axis=-1, keepdims=True)
        log_total = row_max + jnp.log(jnp.sum(jnp.exp(scores - row_max), axis=-1, keepdims=True))
        attn_probs = jnp.exp(scores - log_total).astype(jnp.bfloat16)
        block_out = jnp.einsum(
            "hqk,khd->qhd", attn_probs, values_all, preferred_element_type=jnp.float32
        )
        return (block_out, log_total[..., 0])

    mixed, log_sums = lax.map(one_block, (blocks, starts))
    return (mixed.reshape(key_rows, head_count * head_dim), log_sums)


def attend_backward(queries, keys_all, values_all, mixed_grad, log_sums, slopes, seq_len):
    key_rows, head_count, head_dim = queries.shape
    block_rows, block_count = block_layout(key_rows)
    scale = 1.0 / math.sqrt(head_dim)
    blocks = queries.reshape(block_count, block_rows, head_count, head_dim)
    grad_blocks = mixed_grad.reshape(block_count, block_rows, head_count, head_dim)
    starts = lax.iota(jnp.int32, block_count) * block_rows

    def one_block(carried, inputs):
        key_acc, value_acc = carried
        query_block, grad_block, sum_block, first_row = inputs
        scores = block_scores(query_block, keys_all, first_row, slopes, seq_len)
        attn_probs = jnp.exp(scores - sum_block[..., None])
        prob_grad = jnp.einsum(
            "qhd,khd->hqk", grad_block, values_all, preferred_element_type=jnp.float32
        )
        value_acc = value_acc + jnp.einsum(
            "hqk,qhd->khd",
            attn_probs.astype(jnp.bfloat16),
            grad_block,
            preferred_element_type=jnp.float32,
        )
        row_delta = jnp.sum(attn_probs * prob_grad, axis=-1, keepdims=True)
        score_grad = (attn_probs * (prob_grad - row_delta)).astype(jnp.bfloat16)
        query_grad = (
            jnp.einsum("hqk,khd->qhd", score_grad, keys_all, preferred_element_type=jnp.float32)
            * scale
        )
        key_acc = (
            key_acc
            + jnp.einsum(
                "hqk,qhd->khd", score_grad, query_block, preferred_element_type=jnp.float32
            )
            * scale
        )
        return ((key_acc, value_acc), query_grad)

    zero_acc = jnp.zeros((key_rows, head_count, head_dim), jnp.float32)
    (key_grad, value_grad), query_grad = lax.scan(
        one_block, (zero_acc, zero_acc), (blocks, grad_blocks, log_sums, starts)
    )
    flat_shape = (key_rows, head_count * head_dim)
    return (
        query_grad.reshape(flat_shape),
        key_grad.reshape(flat_shape),
        value_grad.reshape(flat_shape),
    )


def compute(hidden, seq_len, vectors, attn_full, mlp_full):
    gain_one, bias_one, out_bias, gain_two, bias_two, last_bias = vectors
    query_mat, key_mat, value_mat, query_add, value_add, output_mat = attn_full
    up_mat, up_add, down_mat = mlp_full
    local_rows = hidden.shape[0]
    head_count = query_mat.shape[1] // HD
    tensor_id = lax.axis_index("tensor")
    positions = tensor_id * local_rows + lax.iota(jnp.int32, local_rows)
    valid_rows = (positions < seq_len).astype(jnp.float32)[:, None]
    head_ids = (tensor_id * head_count + lax.iota(jnp.int32, head_count) + 1).astype(jnp.float32)
    slopes = jnp.exp2(head_ids * (-8.0 / H))
    hidden_f = hidden.astype(jnp.float32)
    normed_one, unit_one, inverse_one = norm_forward(hidden_f, gain_one, bias_one)
    attn_input = lax.all_gather(normed_one.astype(jnp.bfloat16), "tensor", axis=0, tiled=True)
    key_rows = attn_input.shape[0]
    queries = (
        jnp.dot(attn_input, query_mat, preferred_element_type=jnp.float32) + query_add.reshape(-1)
    ).astype(jnp.bfloat16)
    keys_all = jnp.dot(attn_input, key_mat, preferred_element_type=jnp.float32).astype(jnp.bfloat16)
    values_all = (
        jnp.dot(attn_input, value_mat, preferred_element_type=jnp.float32) + value_add.reshape(-1)
    ).astype(jnp.bfloat16)
    head_shape = (key_rows, head_count, HD)
    queries = queries.reshape(head_shape)
    keys_all = keys_all.reshape(head_shape)
    values_all = values_all.reshape(head_shape)
    mixed_f, log_sums = attend_forward(queries, keys_all, values_all, slopes, seq_len)
    mixed = mixed_f.astype(jnp.bfloat16)
    attn_branch = lax.psum_scatter(
        jnp.dot(mixed, output_mat, preferred_element_type=jnp.float32),
        "tensor",
        scatter_dimension=0,
        tiled=True,
    )
    middle = hidden_f + attn_branch + out_bias
    normed_two, unit_two, inverse_two = norm_forward(middle, gain_two, bias_two)
    mlp_input = lax.all_gather(normed_two.astype(jnp.bfloat16), "tensor", axis=0, tiled=True)
    pre_act = jnp.dot(mlp_input, up_mat, preferred_element_type=jnp.float32) + up_add.reshape(-1)
    act_value, act_slope = gelu_pair(pre_act)
    activated = act_value.astype(jnp.bfloat16)
    mlp_branch = lax.psum_scatter(
        jnp.dot(activated, down_mat, preferred_element_type=jnp.float32).astype(jnp.bfloat16),
        "tensor",
        scatter_dimension=0,
        tiled=True,
    ).astype(jnp.float32)
    layer_out = (valid_rows * (middle + mlp_branch + last_bias)).astype(jnp.bfloat16)
    activations = (
        valid_rows,
        unit_one,
        inverse_one,
        attn_input,
        queries,
        keys_all,
        values_all,
        log_sums,
        mixed,
        unit_two,
        inverse_two,
        mlp_input,
        act_slope,
        activated,
        slopes,
    )
    return (layer_out, activations)


def forward(hidden, seq_len, weights):
    (
        attn_norm_gain,
        attn_norm_bias,
        query_weight,
        key_weight,
        value_weight,
        query_bias,
        value_bias,
        output_weight,
        output_bias,
        mlp_norm_gain,
        mlp_norm_bias,
        up_weight,
        up_bias,
        down_weight,
        down_bias,
    ) = weights
    vectors = (
        lax.all_gather(attn_norm_gain, ("dp", "tensor"), axis=0, tiled=True),
        lax.all_gather(attn_norm_bias, ("dp", "tensor"), axis=0, tiled=True),
        lax.all_gather(output_bias, ("dp", "tensor"), axis=0, tiled=True),
        lax.all_gather(mlp_norm_gain, ("dp", "tensor"), axis=0, tiled=True),
        lax.all_gather(mlp_norm_bias, ("dp", "tensor"), axis=0, tiled=True),
        lax.all_gather(down_bias, ("dp", "tensor"), axis=0, tiled=True),
    )
    attn_full = (
        lax.all_gather(query_weight, "dp", axis=0, tiled=True),
        lax.all_gather(key_weight, "dp", axis=0, tiled=True),
        lax.all_gather(value_weight, "dp", axis=0, tiled=True),
        lax.all_gather(query_bias, "dp", axis=1, tiled=True),
        lax.all_gather(value_bias, "dp", axis=1, tiled=True),
        lax.all_gather(output_weight, "dp", axis=1, tiled=True),
    )
    mlp_full = (
        lax.all_gather(up_weight, "dp", axis=0, tiled=True),
        lax.all_gather(up_bias, "dp", axis=1, tiled=True),
        lax.all_gather(down_weight, "dp", axis=1, tiled=True),
    )
    layer_out, activations = compute(hidden, seq_len, vectors, attn_full, mlp_full)
    return (layer_out, (vectors, attn_full, mlp_full, activations))


def shards(
    hidden,
    seq_lengths,
    attn_norm_gain,
    attn_norm_bias,
    query_weight,
    key_weight,
    value_weight,
    query_bias,
    value_bias,
    output_weight,
    output_bias,
    mlp_norm_gain,
    mlp_norm_bias,
    up_weight,
    up_bias,
    down_weight,
    down_bias,
    out_grad,
):
    weights = (
        attn_norm_gain,
        attn_norm_bias,
        query_weight,
        key_weight,
        value_weight,
        query_bias,
        value_bias,
        output_weight,
        output_bias,
        mlp_norm_gain,
        mlp_norm_bias,
        up_weight,
        up_bias,
        down_weight,
        down_bias,
    )
    seq_len = seq_lengths[0]
    layer_out, stored = forward(hidden, seq_len, weights)
    unused, stored = forward(hidden, seq_len, weights)
    vectors, attn_full, mlp_full, activations = stored
    gain_one, bias_one, out_bias, gain_two, bias_two, last_bias = vectors
    query_mat, key_mat, value_mat, query_add, value_add, output_mat = attn_full
    up_mat, up_add, down_mat = mlp_full
    (
        valid_rows,
        unit_one,
        inverse_one,
        attn_input,
        queries,
        keys_all,
        values_all,
        log_sums,
        mixed,
        unit_two,
        inverse_two,
        mlp_input,
        act_slope,
        activated,
        slopes,
    ) = activations
    upstream = out_grad.astype(jnp.float32) * valid_rows
    last_bias_grad = jnp.sum(upstream, axis=0)
    grad_mlp = lax.all_gather(upstream.astype(jnp.bfloat16), "tensor", axis=0, tiled=True)
    down_grad = dot_rows(activated, grad_mlp)
    pre_grad = (dot_trans(grad_mlp, down_mat) * act_slope).astype(jnp.bfloat16)
    up_add_grad = jnp.sum(pre_grad.astype(jnp.float32), axis=0).reshape(up_add.shape)
    up_grad = dot_rows(mlp_input, pre_grad)
    second_grad = lax.psum_scatter(
        dot_trans(pre_grad, up_mat), "tensor", scatter_dimension=0, tiled=True
    )
    middle_norm_grad, gain_two_grad, bias_two_grad = norm_backward(
        second_grad, unit_two, inverse_two, gain_two
    )
    middle_grad = upstream + middle_norm_grad
    out_bias_grad = jnp.sum(middle_grad, axis=0)
    grad_attn = lax.all_gather(middle_grad.astype(jnp.bfloat16), "tensor", axis=0, tiled=True)
    output_mat_grad = dot_rows(mixed, grad_attn)
    mixed_grad = dot_trans(grad_attn, output_mat).astype(jnp.bfloat16)
    seq_len = seq_lengths[0]
    query_grad, key_grad, value_grad = attend_backward(
        queries, keys_all, values_all, mixed_grad.reshape(queries.shape), log_sums, slopes, seq_len
    )
    query_low = query_grad.astype(jnp.bfloat16)
    key_low = key_grad.astype(jnp.bfloat16)
    value_low = value_grad.astype(jnp.bfloat16)
    query_add_grad = jnp.sum(query_low.astype(jnp.float32), axis=0).reshape(query_add.shape)
    value_add_grad = jnp.sum(value_low.astype(jnp.float32), axis=0).reshape(value_add.shape)
    query_mat_grad = dot_rows(attn_input, query_low)
    key_mat_grad = dot_rows(attn_input, key_low)
    value_mat_grad = dot_rows(attn_input, value_low)
    part_query = dot_trans(query_low, query_mat)
    part_key = dot_trans(key_low, key_mat)
    part_value = dot_trans(value_low, value_mat)
    first_grad = lax.psum_scatter(
        part_query + part_key + part_value, "tensor", scatter_dimension=0, tiled=True
    )
    hidden_norm_grad, gain_one_grad, bias_one_grad = norm_backward(
        first_grad, unit_one, inverse_one, gain_one
    )
    hidden_grad = middle_grad + hidden_norm_grad
    attn_sums = (
        lax.psum_scatter(
            query_mat_grad.astype(jnp.bfloat16), "dp", scatter_dimension=0, tiled=True
        ).astype(jnp.float32),
        lax.psum_scatter(
            key_mat_grad.astype(jnp.bfloat16), "dp", scatter_dimension=0, tiled=True
        ).astype(jnp.float32),
        lax.psum_scatter(
            value_mat_grad.astype(jnp.bfloat16), "dp", scatter_dimension=0, tiled=True
        ).astype(jnp.float32),
        lax.psum_scatter(
            query_add_grad.astype(jnp.bfloat16), "dp", scatter_dimension=1, tiled=True
        ).astype(jnp.float32),
        lax.psum_scatter(
            value_add_grad.astype(jnp.bfloat16), "dp", scatter_dimension=1, tiled=True
        ).astype(jnp.float32),
        lax.psum_scatter(
            output_mat_grad.astype(jnp.bfloat16), "dp", scatter_dimension=1, tiled=True
        ).astype(jnp.float32),
    )
    mlp_sums = (
        lax.psum_scatter(up_grad, "dp", scatter_dimension=0, tiled=True),
        lax.psum_scatter(up_add_grad, "dp", scatter_dimension=1, tiled=True),
        lax.psum_scatter(down_grad, "dp", scatter_dimension=1, tiled=True),
    )
    norm_sums = (
        lax.psum_scatter(gain_one_grad, ("dp", "tensor"), scatter_dimension=0, tiled=True),
        lax.psum_scatter(bias_one_grad, ("dp", "tensor"), scatter_dimension=0, tiled=True),
        lax.psum_scatter(out_bias_grad, ("dp", "tensor"), scatter_dimension=0, tiled=True),
        lax.psum_scatter(gain_two_grad, ("dp", "tensor"), scatter_dimension=0, tiled=True),
        lax.psum_scatter(bias_two_grad, ("dp", "tensor"), scatter_dimension=0, tiled=True),
        lax.psum_scatter(last_bias_grad, ("dp", "tensor"), scatter_dimension=0, tiled=True),
    )
    return (
        layer_out,
        hidden_grad,
        norm_sums[0],
        norm_sums[1],
        attn_sums[0],
        attn_sums[1],
        attn_sums[2],
        attn_sums[3],
        attn_sums[4],
        attn_sums[5],
        norm_sums[2],
        norm_sums[3],
        norm_sums[4],
        mlp_sums[0],
        mlp_sums[1],
        mlp_sums[2],
        norm_sums[5],
    )


def solution(mesh):
    placed = (
        P(("dp", "tensor"), None),
        P("dp"),
        P(("dp", "tensor")),
        P(("dp", "tensor")),
        P("dp", "tensor"),
        P("dp", "tensor"),
        P("dp", "tensor"),
        P("tensor", "dp"),
        P("tensor", "dp"),
        P("tensor", "dp"),
        P(("dp", "tensor")),
        P(("dp", "tensor")),
        P(("dp", "tensor")),
        P("dp", "tensor"),
        P("tensor", "dp"),
        P("tensor", "dp"),
        P(("dp", "tensor")),
        P(("dp", "tensor"), None),
    )
    return jax.shard_map(
        shards,
        mesh=mesh,
        in_specs=placed,
        out_specs=(
            P(("dp", "tensor"), None),
            P(("dp", "tensor"), None),
            P(("dp", "tensor")),
            P(("dp", "tensor")),
            P("dp", "tensor"),
            P("dp", "tensor"),
            P("dp", "tensor"),
            P("tensor", "dp"),
            P("tensor", "dp"),
            P("tensor", "dp"),
            P(("dp", "tensor")),
            P(("dp", "tensor")),
            P(("dp", "tensor")),
            P("dp", "tensor"),
            P("tensor", "dp"),
            P("tensor", "dp"),
            P(("dp", "tensor")),
        ),
        check_vma=False,
    )
```

profile of v0, /device:TPU:0, one launch (start us, length us, event | category | flops | bytes accessed | tf_op | source)
XLA Modules:
  0.0 1980.5 jit_solution(14191513046427565324)
XLA Ops:
  12.3 42.7 %all-reduce.13 = (f32[2048]{0:T(1024)}, f32[2048]{0:T(1024)}, f32[2048]{0:T(1024)S(1)}, f32[2048]{0:T(1024)S(1)}, f32[2048]{0:T(1024)}) all-reduce(f32[2048]{0:T(1024)S(1)} %dynamic-update-slice.4, f32[2048]{0:T(1024)S(1)} %dynamic-update-slice.3, f32[2048]{0:T(1024)S(1)} %dynamic-update-slice.1, ...), channel_id=1, replica_groups=mesh['dp'=8,'tensor'=4] {'dp','tensor'}, use_global_device_ids=true, to_apply=%add.4 | all-reduce | flops 10240 | bytes 81920
  63.3 9.9 all-gather
  73.3 8.0 all-gather.1
  81.5 61.0 %all-gather.14.cloned.1.call-done = bf16[1024,2048]{1,0:T(8,128)(2,1)} async-done(((bf16[256,2048]{1,0:T(8,128)(2,1)}), bf16[1024,2048]{1,0:T(8,128)(2,1)}) %all-gather.14.cloned.1.call-update) | async-done | bytes 4194320 | tf_op jit(solution)/shard_map/all_gather | solution.py:159
  142.5 5.2 add_convert_fusion.2
  148.7 22.1 %all-gather.16.cloned.1.call-done = bf16[2048,512]{1,0:T(8,128)(2,1)} async-done(((bf16[256,512]{1,0:T(8,128)(2,1)}), bf16[2048,512]{1,0:T(8,128)(2,1)}) %all-gather.16.cloned.1.call-update) | async-done | bytes 2097168 | tf_op jit(solution)/shard_map/all_gather | solution.py:240
  170.8 5.2 add_convert_fusion.3
  176.5 24.0 %all-gather.18.cloned.1.call-done = bf16[2048,512]{1,0:T(8,128)(2,1)} async-done(((bf16[256,512]{1,0:T(8,128)(2,1)}), bf16[2048,512]{1,0:T(8,128)(2,1)}) %all-gather.18.cloned.1.call-update) | async-done | bytes 2097168 | tf_op jit(solution)/shard_map/all_gather | solution.py:241
  200.5 6.2 convolution_convert_fusion.5
  209.4 26.1 %while.39 = (s32[]{:T(128)}, bf16[2,512,4,128]{3,1,2,0:T(8,128)(2,1)}, s32[2]{0:T(128)S(1)}, s32[]{:T(128)}, bf16[2,512,4,128]{3,1,2,0:T(8,128)(2,1)S(1)}, /*ind...) while((s32[]{:T(128)}, ...), condition=%wide.region_5.6_spmd.clone, body=%wide.region_2.5_spmd.clone.sunk | while | flops 1111490048 | bytes 47776988 | solution.py:93
  238.5 7.5 fusion.96
  247.2 25.6 %while.40 = (s32[]{:T(128)}, bf16[2,512,4,128]{3,1,2,0:T(8,128)(2,1)}, f32[2,4,512]{2,1,0:T(4,128)S(1)}, s32[2]{0:T(128)S(1)}, s32[]{:T(128)}, /*index=5*/bf16[2...) while((s32[]{:T(128)}, ...), condition=%wide.region_13.14_spmd.clone, body=%wide.region_10.13_spmd.clone.sunk | while | flops 1111490048 | bytes 47785192 | solution.py:93
  276.6 7.2 fusion.94
  284.9 105.8 %reduce-scatter.21.cloned.1.call-done = f32[256,2048]{1,0:T(8,128)} async-done(((f32[1024,2048]{1,0:T(8,128)}), f32[256,2048]{1,0:T(8,128)}) %reduce-scatter.21.cloned.1.call-update) | async-done | bytes 2097168 | tf_op jit(solution)/shard_map/reduce_scatter | solution.py:174
  390.7 147.6 %reduce-scatter.25.cloned.1.call-done = f32[256,2048]{1,0:T(8,128)} async-done(((f32[1024,2048]{1,0:T(8,128)}), f32[256,2048]{1,0:T(8,128)}) %reduce-scatter.25.cloned.1.call-update) | async-done | bytes 2097168 | tf_op jit(solution)/shard_map/reduce_scatter | solution.py:174
  546.5 9.0 all_gather.89
  555.6 39.7 %all-gather.26.cloned.1.call-done = bf16[2048,2048]{1,0:T(8,128)(2,1)} async-done(((bf16[256,2048]{1,0:T(8,128)(2,1)}), bf16[2048,2048]{1,0:T(8,128)(2,1)}) %all-gather.26.cloned.1.call-update) | async-done | bytes 8388624 | tf_op jit(solution)/shard_map/all_gather | solution.py:248
  595.3 82.9 %all-gather.32.cloned.1.call-done = bf16[1024,2048]{1,0:T(8,128)(2,1)} async-done(((bf16[256,2048]{1,0:T(8,128)(2,1)}), bf16[1024,2048]{1,0:T(8,128)(2,1)}) %all-gather.32.cloned.1.call-update) | async-done | bytes 4194320 | tf_op jit(solution)/shard_map/all_gather | solution.py:182
  678.3 14.4 fusion.116
  692.7 66.9 %all-gather.30.cloned.1.call-done = bf16[1024,2048]{1,0:T(8,128)(2,1)} async-done(((bf16[256,2048]{1,0:T(8,128)(2,1)}), bf16[1024,2048]{1,0:T(8,128)(2,1)}) %all-gather.30.cloned.1.call-update) | async-done | bytes 4194320 | tf_op jit(solution)/shard_map/all_gather | solution.py:319
  759.6 56.4 %all-gather.28.cloned.1.call-done = bf16[2048,2048]{1,0:T(8,128)(2,1)} async-done(((bf16[2048,256]{1,0:T(8,128)(2,1)}), bf16[2048,2048]{1,0:T(8,128)(2,1)}) %all-gather.28.cloned.1.call-update) | async-done | bytes 8388624 | tf_op jit(solution)/shard_map/all_gather | solution.py:250
  816.0 18.7 convert_reduce_fusion
  836.7 13.6 fusion.117
  850.4 144.6 %reduce-scatter.27.cloned.1.call-done = f32[256,2048]{1,0:T(8,128)} async-done(((f32[1024,2048]{1,0:T(8,128)}), f32[256,2048]{1,0:T(8,128)}) %reduce-scatter.27.cloned.1.call-update) | async-done | bytes 2097168 | tf_op jit(solution)/shard_map/reduce_scatter | solution.py:324
  1002.5 81.6 %all-gather.34.cloned.1.call-done = bf16[1024,2048]{1,0:T(8,128)(2,1)} async-done(((bf16[256,2048]{1,0:T(8,128)(2,1)}), bf16[1024,2048]{1,0:T(8,128)(2,1)}) %all-gather.34.cloned.1.call-update) | async-done | bytes 4194320 | tf_op jit(solution)/shard_map/all_gather | solution.py:332
  1084.1 6.2 convolution_convert_fusion.4
  1093.9 29.3 %while.41 = (s32[]{:T(128)}, f32[1024,4,128]{0,2,1:T(8,128)S(1)}, f32[1024,4,128]{0,2,1:T(8,128)}, bf16[2,512,4,128]{3,1,2,0:T(8,128)(2,1)}, bf16[2,512,4,128]{3...) while((s32[]{:T(128)}, f32[1024,4,128]{0,2,1:T(8,128)S(1)}, ...), condition=%wide.region_22.23_spmd.clone, body=%wide.region_20.22_spmd.clone.sunk | while | flops 2712403456 | bytes 117490560 | solution.py:135
  1131.1 5.7 add_add_fusion
  1137.5 142.6 %reduce-scatter.29.cloned.1.call-done = f32[256,2048]{1,0:T(8,128)} async-done(((f32[1024,2048]{1,0:T(8,128)}), f32[256,2048]{1,0:T(8,128)}) %reduce-scatter.29.cloned.1.call-update) | async-done | bytes 2097168 | tf_op jit(solution)/shard_map/reduce_scatter | solution.py:350
  1283.4 4.2 fusion.83
  1291.6 6.2 convolution_convert_fusion
  1297.9 6.4 convolution_convert_fusion.1
  1304.4 6.2 convolution_convert_fusion.3
  1310.7 6.3 convolution_convert_fusion.2
  1317.4 51.8 %all-gather.24.cloned.1.call-done = bf16[1024,2048]{1,0:T(8,128)(2,1)} async-done(((bf16[256,2048]{1,0:T(8,128)(2,1)}), bf16[1024,2048]{1,0:T(8,128)(2,1)}) %all-gather.24.cloned.1.call-update) | async-done | bytes 4194320 | tf_op jit(solution)/shard_map/all_gather | solution.py:182
  1369.2 25.9 %fusion.69 = bf16[1024,2048]{1,0:T(8,128)(2,1)} fusion(bf16[2048,2048]{1,0:T(8,128)(2,1)} %all-gather.28.cloned.1.call-done, bf16[1024,2048]{1,0:T(8,128)(2,1)} %all-gather.24.cloned.1.call-done, bf16[2048,2048]{1,0:T(8,128)(2,1)} %all-gather.26.cloned.1.call-done, f32[2048]{0:T(1024)S(1)} %copy-done.48), kind=kOutput, calls=%fused_computation.101 | convolution fusion | flops 17202937856 | bytes 25174016 | tf_op jit(solution)/shard_map/dot_general | solution.py:187
  1395.2 17.2 fusion.54
  1412.7 15.2 fusion.119
  1430.1 9.4 reduce-scatter.43.cloned.1.call-done
  1440.8 33.4 %reduce-scatter.45.cloned.1.call-done = bf16[16,4]{1,0:T(8,128)(2,1)} async-done(((bf16[128,4]{1,0:T(8,128)(2,1)}), bf16[16,4]{1,0:T(8,128)(2,1)}) %reduce-scatter.45.cloned.1.call-update) | async-done | bytes 144
  1475.6 43.6 %reduce-scatter.37.cloned.1.call-done = bf16[512,256]{1,0:T(8,128)(2,1)} async-done(((bf16[512,2048]{1,0:T(8,128)(2,1)}), bf16[512,256]{1,0:T(8,128)(2,1)}) %reduce-scatter.37.cloned.1.call-update) | async-done | bytes 262160 | tf_op jit(solution)/shard_map/reduce_scatter | solution.py:373
  1520.9 42.6 %reduce-scatter.35.cloned.1.call-done = bf16[256,512]{1,0:T(8,128)(2,1)} async-done(((bf16[2048,512]{1,0:T(8,128)(2,1)}), bf16[256,512]{1,0:T(8,128)(2,1)}) %reduce-scatter.35.cloned.1.call-update) | async-done | bytes 262160 | tf_op jit(solution)/shard_map/reduce_scatter | solution.py:364
  1565.3 43.1 %reduce-scatter.31.cloned.1.call-done = bf16[256,512]{1,0:T(8,128)(2,1)} async-done(((bf16[2048,512]{1,0:T(8,128)(2,1)}), bf16[256,512]{1,0:T(8,128)(2,1)}) %reduce-scatter.31.cloned.1.call-update) | async-done | bytes 262160 | tf_op jit(solution)/shard_map/reduce_scatter | solution.py:358
  1610.2 42.7 %reduce-scatter.33.cloned.1.call-done = bf16[256,512]{1,0:T(8,128)(2,1)} async-done(((bf16[2048,512]{1,0:T(8,128)(2,1)}), bf16[256,512]{1,0:T(8,128)(2,1)}) %reduce-scatter.33.cloned.1.call-update) | async-done | bytes 262160 | tf_op jit(solution)/shard_map/reduce_scatter | solution.py:361
  1654.7 43.1 %all-reduce.12 = (f32[2048]{0:T(1024)S(1)}, f32[2048]{0:T(1024)S(1)}, f32[2048]{0:T(1024)S(1)}, f32[2048]{0:T(1024)S(1)}, f32[2048]{0:T(1024)S(1)}, /*index=5*/f32[2048]{0:T(1024)S(1)}, f32[2048]{0:T(1024)S(1)}) all-reduce(f32[2048]{0:T(1024)S(1)} %dynamic-update-slice.5, ...), channel_id=1, replica_groups=mesh['dp'=8,'tensor'=4] {'dp','tensor'}, use_global_device_ids=true, to_apply=%add.5 | all-reduce | flops 14336 | bytes 114688
  1701.4 31.8 %reduce-scatter.23.cloned.1.call-done = bf16[256,2048]{1,0:T(8,128)(2,1)} async-done(((bf16[1024,2048]{1,0:T(8,128)(2,1)}), bf16[256,2048]{1,0:T(8,128)(2,1)}) %reduce-scatter.23.cloned.1.call-update) | async-done | bytes 1048592 | tf_op jit(solution)/shard_map/reduce_scatter | solution.py:186
  1735.9 117.7 %reduce-scatter.41.cloned.1.call-done = f32[2048,256]{1,0:T(8,128)} async-done(((f32[2048,2048]{1,0:T(8,128)}), f32[2048,256]{1,0:T(8,128)}) %reduce-scatter.41.cloned.1.call-update) | async-done | bytes 2097168 | tf_op jit(solution)/shard_map/reduce_scatter | solution.py:380
  1853.7 120.1 %reduce-scatter.39.cloned.1.call-done = f32[256,2048]{1,0:T(8,128)} async-done(((f32[2048,2048]{1,0:T(8,128)}), f32[256,2048]{1,0:T(8,128)}) %reduce-scatter.39.cloned.1.call-update) | async-done | bytes 2097168 | tf_op jit(solution)/shard_map/reduce_scatter | solution.py:378
  (334 shorter events, 161.8 us)
Async XLA Ops:
  7.2 56.2 %copy-start.51 = (bf16[4,16]{1,0:T(4,128)(2,1)S(1)}, bf16[4,16]{1,0:T(4,128)(2,1)}, u32[]{:S(2)}) copy-start(bf16[4,16]{1,0:T(4,128)(2,1)} %param.31) | copy-start | bytes 388
  7.2 66.1 %copy-start.52 = (bf16[4,16]{1,0:T(4,128)(2,1)S(1)}, bf16[4,16]{1,0:T(4,128)(2,1)}, u32[]{:S(2)}) copy-start(bf16[4,16]{1,0:T(4,128)(2,1)} %param.32) | copy-start | bytes 388
  7.2 74.3 %all-gather.20.cloned.1.call-start = ((), (), s32[]{:S(2)}) async-start(), calls=%async_computation.17 | async-start | bytes 2359296 | tf_op jit(solution)/shard_map/all_gather | solution.py:242
  7.9 134.5 %all-gather.14.cloned.1.call-start = ((), (), s32[]{:S(2)}) async-start(), calls=%async_computation.14 | async-start | bytes 5242880 | tf_op jit(solution)/shard_map/all_gather | solution.py:159
  55.0 92.7 %copy-start.32 = (f32[2048]{0:T(1024)}, f32[2048]{0:T(1024)S(1)}, u32[]{:S(2)}) copy-start(f32[2048]{0:T(1024)S(1)} %get-tuple-element.481) | copy-start | bytes 24580
  61.4 109.4 %all-gather.16.cloned.1.call-start = ((), (), s32[]{:S(2)}) async-start(), calls=%async_computation.15 | async-start | bytes 2359296 | tf_op jit(solution)/shard_map/all_gather | solution.py:240
  62.1 138.4 %all-gather.18.cloned.1.call-start = ((), (), s32[]{:S(2)}) async-start(), calls=%async_computation.16 | async-start | bytes 2359296 | tf_op jit(solution)/shard_map/all_gather | solution.py:241
  62.7 175.9 %all-gather.22.cloned.1.call-start = ((), (), s32[]{:S(2)}) async-start(), calls=%async_computation.18 | async-start | bytes 2359296 | tf_op jit(solution)/shard_map/all_gather | solution.py:245
  63.3 327.4 %reduce-scatter.21.cloned.1.call-start = ((), (), s32[]{:S(2)}) async-start(), calls=%async_computation.19 | async-start | bytes 10485760 | tf_op jit(solution)/shard_map/reduce_scatter | solution.py:174
  246.1 292.2 %reduce-scatter.25.cloned.1.call-start = ((), (), s32[]{:S(2)}) async-start(), calls=%async_computation.25 | async-start | bytes 10485760 | tf_op jit(solution)/shard_map/reduce_scatter | solution.py:174
  272.8 11.0 copy-start.9
  283.8 254.4 %copy-start.3 = (bf16[256,2048]{1,0:T(8,128)(2,1)S(1)}, bf16[256,2048]{1,0:T(8,128)(2,1)}, u32[]{:S(2)}) copy-start(bf16[256,2048]{1,0:T(8,128)(2,1)} %param.24) | copy-start | bytes 3145732
  283.8 254.4 %copy-start.28 = (f32[2048]{0:T(1024)S(1)}, f32[2048]{0:T(1024)}, u32[]{:S(2)}) copy-start(f32[2048]{0:T(1024)} %get-tuple-element.482) | copy-start | bytes 24580
  283.9 311.4 %all-gather.26.cloned.1.call-start = ((), (), s32[]{:S(2)}) async-start(), calls=%async_computation.21 | async-start | bytes 9437184 | tf_op jit(solution)/shard_map/all_gather | solution.py:248
  284.6 393.6 %all-gather.32.cloned.1.call-start = ((), (), s32[]{:S(2)}) async-start(), calls=%async_computation.26 | async-start | bytes 5242880 | tf_op jit(solution)/shard_map/all_gather | solution.py:182
  543.6 215.9 %all-gather.30.cloned.1.call-start = ((), (), s32[]{:S(2)}) async-start(), calls=%async_computation.24 | async-start | bytes 5242880 | tf_op jit(solution)/shard_map/all_gather | solution.py:319
  544.4 453.8 %copy-start.42 = (f32[256]{0:T(256)}, f32[256]{0:T(256)S(1)}, u32[]{:S(2)}) copy-start(f32[256]{0:T(256)S(1)} %compare_convert_fusion) | copy-start | bytes 3076
  545.6 270.4 %all-gather.28.cloned.1.call-start = ((), (), s32[]{:S(2)}) async-start(), calls=%async_computation.22 | async-start | bytes 9437184 | tf_op jit(solution)/shard_map/all_gather | solution.py:250
  546.3 448.6 %reduce-scatter.27.cloned.1.call-start = ((), (), s32[]{:S(2)}) async-start(), calls=%async_computation.27 | async-start | bytes 10485760 | tf_op jit(solution)/shard_map/reduce_scatter | solution.py:324
  555.6 260.4 %copy-start.47 = (f32[2048]{0:T(1024)}, f32[2048]{0:T(1024)S(1)}, u32[]{:S(2)}) copy-start(f32[2048]{0:T(1024)S(1)} %bitcast_convert_fusion) | copy-start | bytes 24580
  850.3 233.8 %all-gather.34.cloned.1.call-start = ((), (), s32[]{:S(2)}) async-start(), calls=%async_computation.28 | async-start | bytes 5242880 | tf_op jit(solution)/shard_map/all_gather | solution.py:332
  1002.4 277.6 %reduce-scatter.29.cloned.1.call-start = ((), (), s32[]{:S(2)}) async-start(), calls=%async_computation.29 | async-start | bytes 10485760 | tf_op jit(solution)/shard_map/reduce_scatter | solution.py:350
  1002.5 91.4 %copy-start.6 = (bf16[1024,4,128]{2,0,1:T(8,128)(2,1)S(1)}, bf16[1024,4,128]{2,0,1:T(8,128)(2,1)}, u32[]{:S(2)}) copy-start(bf16[1024,4,128]{2,0,1:T(8,128)(2,1)} %copy-done.5) | copy-start | bytes 3145732
  1136.8 143.2 %copy-start.4 = (bf16[256,2048]{1,0:T(8,128)(2,1)S(1)}, bf16[256,2048]{1,0:T(8,128)(2,1)}, u32[]{:S(2)}) copy-start(bf16[256,2048]{1,0:T(8,128)(2,1)} %param.24) | copy-start | bytes 3145732
  1136.8 143.2 %copy-start.11 = (f32[256,2048]{1,0:T(8,128)S(1)}, f32[256,2048]{1,0:T(8,128)}, u32[]{:S(2)}) copy-start(f32[256,2048]{1,0:T(8,128)} %reduce-scatter.21.cloned.1.call-done) | copy-start | bytes 6291460
  1136.8 143.2 %copy-start.29 = (f32[2048]{0:T(1024)S(1)}, f32[2048]{0:T(1024)}, u32[]{:S(2)}) copy-start(f32[2048]{0:T(1024)} %get-tuple-element.482) | copy-start | bytes 24580
  1136.8 143.2 %copy-start.33 = (f32[2048]{0:T(1024)S(1)}, f32[2048]{0:T(1024)}, u32[]{:S(2)}) copy-start(f32[2048]{0:T(1024)} %copy-done.32) | copy-start | bytes 24580
  1136.8 143.2 %copy-start.41 = (f32[256]{0:T(256)S(1)}, f32[256]{0:T(256)}, u32[]{:S(2)}) copy-start(f32[256]{0:T(256)} %copy-done.40) | copy-start | bytes 3076
  1136.8 143.2 %copy-start.45 = (f32[256]{0:T(256)S(1)}, f32[256]{0:T(256)}, u32[]{:S(2)}) copy-start(f32[256]{0:T(256)} %copy-done.44) | copy-start | bytes 3076
  1136.9 146.5 %copy-start.31 = (f32[2048]{0:T(1024)S(1)}, f32[2048]{0:T(1024)}, u32[]{:S(2)}) copy-start(f32[2048]{0:T(1024)} %get-tuple-element.479) | copy-start | bytes 24580
  1136.9 146.5 %copy-start.37 = (f32[2048]{0:T(1024)S(1)}, f32[2048]{0:T(1024)}, u32[]{:S(2)}) copy-start(f32[2048]{0:T(1024)} %get-tuple-element.478) | copy-start | bytes 24580
  1136.9 232.3 %all-gather.24.cloned.1.call-start = ((), (), s32[]{:S(2)}) async-start(), calls=%async_computation.20 | async-start | bytes 5242880 | tf_op jit(solution)/shard_map/all_gather | solution.py:182
  1287.6 141.2 %reduce-scatter.47.cloned.1.call-start = ((), (), s32[]{:S(2)}) async-start(), calls=%async_computation.38 | async-start | bytes 73728
  1288.4 151.1 %reduce-scatter.43.cloned.1.call-start = ((), (), s32[]{:S(2)}) async-start(), calls=%async_computation.36 | async-start | bytes 36864
  1290.6 183.6 %reduce-scatter.45.cloned.1.call-start = ((), (), s32[]{:S(2)}) async-start(), calls=%async_computation.37 | async-start | bytes 36864
  1291.4 227.7 %reduce-scatter.37.cloned.1.call-start = ((), (), s32[]{:S(2)}) async-start(), calls=%async_computation.33 | async-start | bytes 2359296 | tf_op jit(solution)/shard_map/reduce_scatter | solution.py:373
  1297.9 265.6 %reduce-scatter.35.cloned.1.call-start = ((), (), s32[]{:S(2)}) async-start(), calls=%async_computation.32 | async-start | bytes 2359296 | tf_op jit(solution)/shard_map/reduce_scatter | solution.py:364
  1304.4 304.0 %reduce-scatter.31.cloned.1.call-start = ((), (), s32[]{:S(2)}) async-start(), calls=%async_computation.30 | async-start | bytes 2359296 | tf_op jit(solution)/shard_map/reduce_scatter | solution.py:358
  1310.6 58.6 %copy-start.48 = (f32[2048]{0:T(1024)S(1)}, f32[2048]{0:T(1024)}, u32[]{:S(2)}) copy-start(f32[2048]{0:T(1024)} %copy-done.47) | copy-start | bytes 24580
  1310.6 342.3 %reduce-scatter.33.cloned.1.call-start = ((), (), s32[]{:S(2)}) async-start(), calls=%async_computation.31 | async-start | bytes 2359296 | tf_op jit(solution)/shard_map/reduce_scatter | solution.py:361
  1317.0 416.2 %reduce-scatter.23.cloned.1.call-start = ((), (), s32[]{:S(2)}) async-start(), calls=%async_computation.23 | async-start | bytes 5242880 | tf_op jit(solution)/shard_map/reduce_scatter | solution.py:186
  1395.2 458.5 %reduce-scatter.41.cloned.1.call-start = ((), (), s32[]{:S(2)}) async-start(), calls=%async_computation.35 | async-start | bytes 18874368 | tf_op jit(solution)/shard_map/reduce_scatter | solution.py:380
  1412.4 561.3 %reduce-scatter.39.cloned.1.call-start = ((), (), s32[]{:S(2)}) async-start(), calls=%async_computation.34 | async-start | bytes 18874368 | tf_op jit(solution)/shard_map/reduce_scatter | solution.py:378
  1427.9 226.8 %copy-start.34 = (f32[2048]{0:T(1024)S(1)}, f32[2048]{0:T(1024)}, u32[]{:S(2)}) copy-start(f32[2048]{0:T(1024)} %get-tuple-element.404) | copy-start | bytes 24580
  1427.9 226.8 %copy-start.35 = (f32[2048]{0:T(1024)S(1)}, f32[2048]{0:T(1024)}, u32[]{:S(2)}) copy-start(f32[2048]{0:T(1024)} %get-tuple-element.410) | copy-start | bytes 24580
  1427.9 226.8 %copy-start.38 = (f32[2048]{0:T(1024)S(1)}, f32[2048]{0:T(1024)}, u32[]{:S(2)}) copy-start(f32[2048]{0:T(1024)} %get-tuple-element.487) | copy-start | bytes 24580
  1427.9 226.8 %copy-start.39 = (f32[2048]{0:T(1024)S(1)}, f32[2048]{0:T(1024)}, u32[]{:S(2)}) copy-start(f32[2048]{0:T(1024)} %get-tuple-element.498) | copy-start | bytes 24580
  1427.9 305.2 %copy-start.43 = (f32[256]{0:T(256)S(1)}, f32[256]{0:T(256)}, u32[]{:S(2)}) copy-start(f32[256]{0:T(256)} %copy-done.42) | copy-start | bytes 3076
  (44 other events, 117.3 us)
Sparse Core Ops, SparseCore 0:
  9.9 30.8 all-gather.19
  61.5 80.9 all-gather.13
  144.4 26.4 all-gather.15
  172.6 27.8 all-gather.17
  202.2 28.1 all-gather.21
  246.2 144.4 reduce-scatter.20
  393.0 145.1 reduce-scatter.24
  540.1 55.1 all-gather.25
  597.5 80.7 all-gather.31
  680.3 79.2 all-gather.29
  761.5 54.4 all-gather.27
  850.4 144.4 reduce-scatter.26
  1002.6 81.4 all-gather.33
  1137.0 143.0 reduce-scatter.28
  1287.7 81.4 all-gather.23
  1372.6 31.7 reduce-scatter.46
  1408.1 31.2 reduce-scatter.42
  1442.9 31.2 reduce-scatter.44
  1477.8 41.2 reduce-scatter.36
  1522.2 41.1 reduce-scatter.34
  1567.1 41.2 reduce-scatter.30
  1611.6 41.1 reduce-scatter.32
  1655.3 77.8 reduce-scatter.22
  1737.1 116.4 reduce-scatter.40
  1857.8 115.9 reduce-scatter.38
where the time goes:
time: 1990 us; the launch traced here: 1980 us
  waiting for transfers between devices  1520 us (76%)
  matrix products  221 us (11%)
  blocking collectives  113 us (6%)
  other arithmetic  64.1 us (3%)
  local copies, waits for them, and re-layouts  48.4 us (2%)
    reduce_scatter x2, waiting for transfers between devices, compute(): lax.psum_scatter(jnp.dot(mixed, output_mat, preferred_element_type=jnp.fl...  253 us
    reduce_scatter x1, waiting for transfers between devices, shards(): lax.psum_scatter(dot_trans(pre_grad, up_mat), 'tensor', scatter_dimension...  145 us
    reduce_scatter x1, waiting for transfers between devices, shards(): lax.psum_scatter(part_query + part_key + part_value, 'tensor', scatter_di...  143 us
    all_gather x2, waiting for transfers between devices, compute(): lax.all_gather(normed_two.astype(jnp.bfloat16), 'tensor', axis=0, tiled=T...  135 us
    reduce_scatter x1, waiting for transfers between devices, shards(): lax.psum_scatter(up_grad, 'dp', scatter_dimension=0, tiled=True)  120 us
    reduce_scatter x1, waiting for transfers between devices, shards(): lax.psum_scatter(down_grad, 'dp', scatter_dimension=1, tiled=True)  118 us
    unnamed x2, blocking collectives  85.9 us
    all_gather x1, waiting for transfers between devices, shards(): lax.all_gather(middle_grad.astype(jnp.bfloat16), 'tensor', axis=0, tiled=...  81.6 us
  transfers between devices with their start and end apart: 25, of which 22 were waited for; matrix products, arithmetic and copies ran while one was open for 11% of the time, Pallas kernels for 0%

commit v1 on v0

v1 whole, which is shorter than its diff:
```python
import functools
import math

import jax
import jax.numpy as jnp
from jax import lax
from jax.experimental import pallas as pl
from jax.experimental.pallas import tpu as pltpu
from jax.sharding import PartitionSpec as P

H = 16
HD = 128
EPSILON = 1e-05
GELU_COEF = math.sqrt(2.0 / math.pi)
NEGATIVE = -1e30
MESH = pl.DeviceIdType.MESH
F32 = jnp.float32
BF16 = jnp.bfloat16
MIB = 1024 * 1024


def norm_parts(values):
    center = values - jnp.mean(values, axis=-1, keepdims=True)
    inverse = lax.rsqrt(jnp.mean(center * center, axis=-1, keepdims=True) + EPSILON)
    return (center * inverse, inverse)


def norm_backward(upstream, unit, inverse, gain):
    scaled = upstream * gain
    return inverse * (
        scaled
        - jnp.mean(scaled, axis=-1, keepdims=True)
        - unit * jnp.mean(scaled * unit, axis=-1, keepdims=True)
    )


def gelu_pair(values):
    squared = values * values
    tanh_val = jnp.tanh(GELU_COEF * (values + 0.044715 * values * squared))
    half = 0.5 * (1.0 + tanh_val)
    slope = half + 0.5 * values * (1.0 - tanh_val * tanh_val) * GELU_COEF * (
        1.0 + 3.0 * 0.044715 * squared
    )
    return (values * half, slope)


def dot(left, right):
    return jnp.dot(left, right, preferred_element_type=F32)


def dot_rows(left, right):
    return lax.dot_general(left, right, (((0,), (0,)), ((), ())), preferred_element_type=F32)


def dot_trans(left, right):
    return lax.dot_general(left, right, (((1,), (1,)), ((), ())), preferred_element_type=F32)


def flip(index, bit):
    return index + bit - 2 * bit * ((index // bit) % 2)


def remote(src, dst, send_sem, recv_sem, device):
    return pltpu.make_async_remote_copy(
        src_ref=src,
        dst_ref=dst,
        send_sem=send_sem,
        recv_sem=recv_sem,
        device_id=device,
        device_id_type=MESH,
    )


def greet(n, plane):
    z = lax.axis_index("tensor")
    barrier = pltpu.get_barrier_semaphore()

    @pl.when(z > 0)
    def _():
        pl.semaphore_signal(barrier, inc=1, device_id={"tensor": z - 1}, device_id_type=MESH)

    @pl.when(z < n - 1)
    def _():
        pl.semaphore_signal(barrier, inc=1, device_id={"tensor": z + 1}, device_id_type=MESH)

    if plane:
        p = lax.axis_index("dp")
        for partner in (flip(p, 1), flip(p, 2), flip(p, 4), flip(flip(p, 2), 4)):
            pl.semaphore_signal(barrier, inc=1, device_id={"dp": partner}, device_id_type=MESH)

    peers = jnp.minimum(z, 1) + jnp.minimum(n - 1 - z, 1)
    pl.semaphore_wait(barrier, peers + 4 if plane else peers)


def gather_body(
    n, cut, hid, og, wq, wk, wv, wo, up, down,
    hid_all, og_all, wqkv_all, wo_all, up_all, down_all,
    zsend, zrecv, wsend, wrecv, lsem,
):
    z = lax.axis_index("tensor")
    p = lax.axis_index("dp")
    piece = hid.shape[0] // cut
    shards = (wq, wk, wv, wo, up, down)
    part, width = wq.shape
    evens = {2: flip(p, 2), 4: flip(p, 4), 6: flip(flip(p, 2), 4)}
    sibling = flip(p, 1)
    zin = (hid, og)
    zout = (hid_all, og_all)

    def slot(i, q):
        if i < 3:
            return wqkv_all.at[pl.ds(q * part, part), pl.ds(i * width, width)]
        if i == 3:
            return wo_all.at[:, pl.ds(q * part, part)]
        if i == 4:
            return up_all.at[pl.ds(q * part, part), :]
        return down_all.at[:, pl.ds(q * part, part)]

    def direct(i, q):
        return remote(shards[i], slot(i, p), wsend.at[i, q], wrecv.at[i, q], {"dp": evens[q]})

    def relay(i, q):
        owner = p if q == 0 else evens[q]
        src = shards[i] if q == 0 else slot(i, owner)
        return remote(src, slot(i, owner), wsend.at[i, q + 1], wrecv.at[i, q + 1], {"dp": sibling})

    def zcopy(a, way, k, c, shard):
        to = z + 1 if way == 0 else z - 1
        rows = pl.ds(c * piece, piece)
        src = zin[a].at[rows, :] if k == 0 else zout[a].at[shard, rows, :]
        dst = zout[a].at[shard, rows, :]
        return remote(src, dst, zsend.at[a, way, k, c], zrecv.at[a, way, k, c], {"tensor": to})

    def zsend_hop(a, k, c):
        @pl.when(jnp.logical_and(z >= k, z <= n - 2))
        def _():
            zcopy(a, 0, k, c, z - k).start()

        @pl.when(jnp.logical_and(z + k <= n - 1, z >= 1))
        def _():
            zcopy(a, 1, k, c, z + k).start()

    def zstep(a, k):
        for c in range(cut):
            @pl.when(z >= k)
            def _():
                zcopy(a, 0, k - 1, c, z - k).wait_recv()

            @pl.when(z + k <= n - 1)
            def _():
                zcopy(a, 1, k - 1, c, z + k).wait_recv()

            if k < n - 1:
                zsend_hop(a, k, c)

    def zdrain(a):
        for k in range(n - 1):
            for c in range(cut):
                @pl.when(jnp.logical_and(z >= k, z <= n - 2))
                def _():
                    zcopy(a, 0, k, c, z - k).wait_send()

                @pl.when(jnp.logical_and(z + k <= n - 1, z >= 1))
                def _():
                    zcopy(a, 1, k, c, z + k).wait_send()

    def forward(i):
        for q in (2, 4, 6):
            direct(i, q).wait_recv()
            relay(i, q).start()

    greet(n, True)
    for c in range(cut):
        zsend_hop(0, 0, c)
    for i in range(6):
        for q in (2, 4, 6):
            direct(i, q).start()
        relay(i, 0).start()
    for c in range(cut):
        zsend_hop(1, 0, c)
    local = [pltpu.make_async_copy(zin[a], zout[a].at[z], lsem.at[a]) for a in range(2)]
    local += [pltpu.make_async_copy(shards[i], slot(i, p), lsem.at[2 + i]) for i in range(6)]
    for copy in local:
        copy.start()
    zstep(0, 1)
    forward(0)
    forward(1)
    forward(2)
    for k in range(2, n):
        zstep(0, k)
        zstep(1, k - 1)
    forward(3)
    forward(4)
    zstep(1, n - 1)
    forward(5)
    for i in range(6):
        for q in (0, 2, 4, 6):
            relay(i, q).wait_recv()
    for i in range(6):
        for q in (2, 4, 6):
            direct(i, q).wait_send()
        for q in (0, 2, 4, 6):
            relay(i, q).wait_send()
    zdrain(0)
    zdrain(1)
    for copy in local:
        copy.wait()


def gather_inputs(n, hid, og, weights, cut=2):
    wq, _, _, wo, up, down = weights
    rows, d = hid.shape
    dp = lax.axis_size("dp")
    if dp != 8:
        along = lambda w, axis: lax.all_gather(w, "dp", axis=axis, tiled=True)
        wqkv = jnp.concatenate(weights[:3], axis=1)
        return (
            lax.all_gather(hid, "tensor"),
            lax.all_gather(og, "tensor"),
            along(wqkv, 0),
            along(wo, 1),
            along(up, 0),
            along(down, 1),
        )
    out = lambda *shape: jax.ShapeDtypeStruct(shape, BF16)
    return pl.pallas_call(
        functools.partial(gather_body, n, cut),
        out_shape=(
            out(n, rows, d),
            out(n, rows, d),
            out(wq.shape[0] * dp, 3 * wq.shape[1]),
            out(wo.shape[0], wo.shape[1] * dp),
            out(up.shape[0] * dp, up.shape[1]),
            out(down.shape[0], down.shape[1] * dp),
        ),
        in_specs=[pl.BlockSpec(memory_space=pltpu.VMEM)] * 8,
        out_specs=[pl.BlockSpec(memory_space=pl.ANY)] * 6,
        scratch_shapes=[
            pltpu.SemaphoreType.DMA((2, 2, n - 1, cut)),
            pltpu.SemaphoreType.DMA((2, 2, n - 1, cut)),
            pltpu.SemaphoreType.DMA((6, 8)),
            pltpu.SemaphoreType.DMA((6, 8)),
            pltpu.SemaphoreType.DMA((8,)),
        ],
        compiler_params=pltpu.CompilerParams(
            collective_id=0, has_side_effects=True, vmem_limit_bytes=16 * MIB
        ),
        name="gather_inputs",
    )(hid, og, *weights)


def block_scores(query_block, keys_all, first_row, slopes, seq_len):
    block_rows = query_block.shape[0]
    key_rows = keys_all.shape[0]
    scale = 1.0 / math.sqrt(HD)
    scores = jnp.einsum("qhd,khd->hqk", query_block, keys_all, preferred_element_type=F32) * scale
    query_pos = first_row + lax.iota(jnp.int32, block_rows)
    key_pos = lax.iota(jnp.int32, key_rows)
    distance = (query_pos[:, None] - key_pos[None, :]).astype(F32)
    scores = scores - slopes[:, None, None] * distance
    allowed = (key_pos[None, :] <= query_pos[:, None]) & (key_pos[None, :] < seq_len)
    return jnp.where(allowed[None], scores, NEGATIVE)


def attend_forward(queries, keys_all, values_all, slopes, seq_len):
    key_rows, head_count, head_dim = queries.shape
    block_rows = min(512, key_rows)
    block_count = key_rows // block_rows
    blocks = queries.reshape(block_count, block_rows, head_count, head_dim)
    starts = lax.iota(jnp.int32, block_count) * block_rows

    def one_block(inputs):
        query_block, first_row = inputs
        scores = block_scores(query_block, keys_all, first_row, slopes, seq_len)
        row_max = jnp.max(scores, axis=-1, keepdims=True)
        log_total = row_max + jnp.log(jnp.sum(jnp.exp(scores - row_max), axis=-1, keepdims=True))
        attn_probs = jnp.exp(scores - log_total).astype(BF16)
        block_out = jnp.einsum("hqk,khd->qhd", attn_probs, values_all, preferred_element_type=F32)
        return (block_out, log_total[..., 0])

    mixed, log_sums = lax.map(one_block, (blocks, starts))
    return (mixed.reshape(key_rows, head_count * head_dim), log_sums)


def attend_backward(queries, keys_all, values_all, mixed_grad, log_sums, slopes, seq_len):
    key_rows, head_count, head_dim = queries.shape
    block_rows = min(512, key_rows)
    block_count = key_rows // block_rows
    scale = 1.0 / math.sqrt(head_dim)
    blocks = queries.reshape(block_count, block_rows, head_count, head_dim)
    grad_blocks = mixed_grad.reshape(block_count, block_rows, head_count, head_dim)
    starts = lax.iota(jnp.int32, block_count) * block_rows

    def one_block(carried, inputs):
        key_acc, value_acc = carried
        query_block, grad_block, sum_block, first_row = inputs
        scores = block_scores(query_block, keys_all, first_row, slopes, seq_len)
        attn_probs = jnp.exp(scores - sum_block[..., None])
        prob_grad = jnp.einsum("qhd,khd->hqk", grad_block, values_all, preferred_element_type=F32)
        value_acc = value_acc + jnp.einsum(
            "hqk,qhd->khd", attn_probs.astype(BF16), grad_block, preferred_element_type=F32
        )
        row_delta = jnp.sum(attn_probs * prob_grad, axis=-1, keepdims=True)
        score_grad = (attn_probs * (prob_grad - row_delta)).astype(BF16)
        query_grad = (
            jnp.einsum("hqk,khd->qhd", score_grad, keys_all, preferred_element_type=F32) * scale
        )
        key_acc = (
            key_acc
            + jnp.einsum("hqk,qhd->khd", score_grad, query_block, preferred_element_type=F32)
            * scale
        )
        return ((key_acc, value_acc), query_grad)

    zero_acc = jnp.zeros((key_rows, head_count, head_dim), F32)
    (key_grad, value_grad), query_grad = lax.scan(
        one_block, (zero_acc, zero_acc), (blocks, grad_blocks, log_sums, starts)
    )
    flat = (key_rows, head_count * head_dim)
    return (query_grad.reshape(flat), key_grad.reshape(flat), value_grad.reshape(flat))


def scatter_rows(partial_sum):
    return lax.psum_scatter(
        partial_sum.astype(BF16), "tensor", scatter_dimension=0, tiled=True
    ).astype(F32)


def gather_rows(rows):
    return lax.all_gather(rows.astype(BF16), "tensor", axis=0, tiled=True)


def middle_part(n, mixed, wo, up, down, up_add, out_bias, gain_two, bias_two, hidden_f, upstream, og_low):
    middle = hidden_f + scatter_rows(dot(mixed, wo)) + out_bias
    unit_two, inverse_two = norm_parts(middle)
    mlp_input = gather_rows(unit_two * gain_two + bias_two)
    act_value, act_slope = gelu_pair(dot(mlp_input, up) + up_add)
    activated = act_value.astype(BF16)
    mlp_partial = dot(activated, down).astype(BF16)
    pre_grad = (dot_trans(og_low, down) * act_slope).astype(BF16)
    second_grad = scatter_rows(dot_trans(pre_grad, up))
    middle_grad = upstream + norm_backward(second_grad, unit_two, inverse_two, gain_two)
    grad_attn = gather_rows(middle_grad)
    mixed_grad = dot_trans(grad_attn, wo).astype(BF16)
    sums = (jnp.sum(second_grad * unit_two, axis=0), jnp.sum(second_grad, axis=0))
    return (middle, mlp_input, activated, mlp_partial, pre_grad, middle_grad, grad_attn, mixed_grad, sums)


def shards(
    hidden, seq_lengths, attn_norm_gain, attn_norm_bias, query_weight, key_weight, value_weight,
    query_bias, value_bias, output_weight, output_bias, mlp_norm_gain, mlp_norm_bias, up_weight,
    up_bias, down_weight, down_bias, out_grad,
):
    n = lax.axis_size("tensor")
    dp = lax.axis_size("dp")
    z = lax.axis_index("tensor")
    rows, d = hidden.shape
    heads, hd_part = query_bias.shape
    up_heads = up_bias.shape[0]
    width = query_weight.shape[1]
    seq_len = seq_lengths[0]
    valid = (z * rows + lax.iota(jnp.int32, rows) < seq_len).astype(F32)[:, None]

    vec = attn_norm_gain.shape[0]
    heads_all = 2 * heads + up_heads
    packed = jnp.concatenate(
        [
            jnp.stack(
                [attn_norm_gain, attn_norm_bias, output_bias, mlp_norm_gain, mlp_norm_bias, down_bias]
            ).reshape(-1),
            jnp.concatenate([query_bias, value_bias, up_bias]).astype(F32).reshape(-1),
        ]
    )
    packed = lax.all_gather(packed, ("dp", "tensor"), axis=0)
    vectors = packed[:, : 6 * vec].reshape(dp * n, 6, vec).transpose(1, 0, 2).reshape(6, d)
    gain_one, bias_one, out_bias, gain_two, bias_two, last_bias = (vectors[i] for i in range(6))
    biases = lax.dynamic_index_in_dim(
        packed[:, 6 * vec :].reshape(dp, n, heads_all, hd_part), z, 1, keepdims=False
    )
    biases = biases.transpose(1, 0, 2).reshape(heads_all * HD)
    query_add, value_add, up_add = (
        biases[:width],
        biases[width : 2 * width],
        biases[2 * width :],
    )

    upstream = out_grad.astype(F32) * valid
    hid_all, og_all, wqkv, wo, up, down = gather_inputs(
        n,
        hidden,
        upstream.astype(BF16),
        (query_weight, key_weight, value_weight, output_weight, up_weight, down_weight),
    )
    key_rows = n * rows
    og_low = og_all.reshape(key_rows, d)
    head_ids = (z * heads + lax.iota(jnp.int32, heads) + 1).astype(F32)
    slopes = jnp.exp2(head_ids * (-8.0 / H))

    unit_all, _ = norm_parts(hid_all.reshape(key_rows, d).astype(F32))
    attn_input = (unit_all * gain_one + bias_one).astype(BF16)
    qkv_add = jnp.concatenate([query_add, jnp.zeros_like(query_add), value_add])
    qkv = (dot(attn_input, wqkv) + qkv_add).astype(BF16)
    queries, keys_all, values_all = (
        qkv[:, i * width : (i + 1) * width].reshape(key_rows, heads, HD) for i in range(3)
    )
    mixed_f, log_sums = attend_forward(queries, keys_all, values_all, slopes, seq_len)
    mixed = mixed_f.astype(BF16)

    hidden_f = hidden.astype(F32)
    middle, mlp_input, activated, mlp_partial, pre_grad, middle_grad, grad_attn, mixed_grad, sums = (
        middle_part(
            n, mixed, wo, up, down, up_add, out_bias, gain_two, bias_two, hidden_f, upstream, og_low
        )
    )
    gain_two_grad, bias_two_grad = sums
    mlp_branch = lax.psum_scatter(mlp_partial, "tensor", scatter_dimension=0, tiled=True)
    layer_out = (valid * (middle + mlp_branch.astype(F32) + last_bias)).astype(BF16)

    down_grad = dot_rows(activated, og_low)
    up_grad = dot_rows(mlp_input, pre_grad)
    up_add_grad = jnp.sum(pre_grad.astype(F32), axis=0)
    out_grad_mat = dot_rows(mixed, grad_attn)

    query_grad, key_grad, value_grad = attend_backward(
        queries, keys_all, values_all, mixed_grad.reshape(queries.shape), log_sums, slopes, seq_len
    )
    qkv_grad = jnp.concatenate([query_grad, key_grad, value_grad], axis=1).astype(BF16)
    qkv_mat_grad = dot_rows(attn_input, qkv_grad)
    qkv_add_grad = jnp.sum(qkv_grad.astype(F32), axis=0)
    first_grad = scatter_rows(dot_trans(qkv_grad, wqkv))
    unit_one, inverse_one = norm_parts(hidden_f)
    hidden_grad = middle_grad + norm_backward(first_grad, unit_one, inverse_one, gain_one)

    over_dp = lambda w, axis: lax.psum_scatter(
        w.astype(BF16), "dp", scatter_dimension=axis, tiled=True
    ).astype(F32)
    qkv_out = over_dp(qkv_mat_grad, 0)
    query_out, key_out, value_out = (qkv_out[:, i * width : (i + 1) * width] for i in range(3))
    wo_out = over_dp(out_grad_mat, 1)
    up_out = over_dp(up_grad, 0)
    down_out = over_dp(down_grad, 1)
    vec_grads = jnp.stack(
        [
            jnp.sum(first_grad * unit_one, axis=0),
            jnp.sum(first_grad, axis=0),
            jnp.sum(middle_grad, axis=0),
            gain_two_grad,
            bias_two_grad,
            jnp.sum(upstream, axis=0),
        ]
    )
    vec_grads = vec_grads.reshape(6, dp * n, vec).transpose(1, 0, 2).reshape(dp, n, 6 * vec)
    bias_grads = jnp.concatenate([qkv_add_grad[:width], qkv_add_grad[2 * width :], up_add_grad])
    bias_grads = bias_grads.reshape(heads_all, dp, hd_part).transpose(1, 0, 2).reshape(dp, 1, -1)
    mine = (lax.iota(jnp.int32, n) == z).astype(F32)[None, :, None]
    small = jnp.concatenate([vec_grads, bias_grads * mine], axis=2).reshape(dp * n, -1)
    small = lax.psum_scatter(small, ("dp", "tensor"), scatter_dimension=0, tiled=True)[0]
    vec_out = small[: 6 * vec].reshape(6, vec)
    bias_out = small[6 * vec :].reshape(heads_all, hd_part)
    return (
        layer_out,
        hidden_grad,
        vec_out[0],
        vec_out[1],
        query_out,
        key_out,
        value_out,
        bias_out[:heads],
        bias_out[heads : 2 * heads],
        wo_out,
        vec_out[2],
        vec_out[3],
        vec_out[4],
        up_out,
        bias_out[2 * heads :],
        down_out,
        vec_out[5],
    )


def solution(mesh):
    vector = P(("dp", "tensor"))
    rows = P(("dp", "tensor"), None)
    wide = P("dp", "tensor")
    tall = P("tensor", "dp")
    return jax.shard_map(
        shards,
        mesh=mesh,
        in_specs=(
            rows, P("dp"), vector, vector, wide, wide, wide, tall, tall, tall, vector, vector,
            vector, wide, tall, tall, vector, rows,
        ),
        out_specs=(
            rows, rows, vector, vector, wide, wide, wide, tall, tall, tall, vector, vector,
            vector, wide, tall, tall, vector,
        ),
        check_vma=False,
    )
```

time: 1990 us -> 1320 us (0.66)
  waiting for transfers between devices: 1520 us -> 764 us
  Pallas kernels: 0 us -> 147 us
  blocking collectives: 113 us -> 68.1 us
  matrix products: 221 us -> 193 us
    reduce_scatter x11 -> x8, waiting for transfers between devices: 982 us -> 479 us  [the longest x4 237 us: shards(): lax.psum_scatter(w.astype(BF16), 'dp', scatter_dimension=axis, tiled=True)]
    all_gather x11 -> x2, waiting for transfers between devices: 486 us -> 162 us  [gather_rows(): return lax.all_gather(rows.astype(BF16), 'tensor', axis=0, tiled=True)]
    pallas_call x0 -> x1, Pallas kernels: none -> 147 us  [gather_inputs(): pl.pallas_call(functools.partial(gather_body, n, cut), out_shape=(out(n,...]
    unnamed x2 -> x0, blocking collectives: 85.9 us -> none
    unnamed x28 -> x12, waiting for transfers between devices: 46.9 us -> 123 us
    all_gather x3 -> x1, blocking collectives: 27 us -> 68.1 us  [shards(): packed = lax.all_gather(packed, ('dp', 'tensor'), axis=0)]
    dot_general x23 -> x16, matrix products: 183 us -> 153 us  [the longest x4 47.5 us: dot_trans(): lax.dot_general(left, right, (((1,), (1,)), ((), ())), preferred_element_...]
  transfers between devices with their start and end apart: 25 -> 11, of which waited for: 22 -> 11; matrix products, arithmetic and copies ran while one was open for 11% -> 7% of each run, Pallas kernels for 0% -> 0%
where the time goes in v1:
time: 1320 us; the launch traced here: 1310 us
  waiting for transfers between devices  764 us (58%)
  matrix products  193 us (15%)
  Pallas kernels  147 us (11%)
  blocking collectives  68.1 us (5%)
  local copies, waits for them, and re-layouts  59.8 us (5%)
  other arithmetic  58.8 us (4%)
  between operations  15.4 us (1%)
    reduce_scatter x4, waiting for transfers between devices, shards(): lax.psum_scatter(w.astype(BF16), 'dp', scatter_dimension=axis, tiled=True)  237 us
    reduce_scatter x3, waiting for transfers between devices, scatter_rows(): lax.psum_scatter(partial_sum.astype(BF16), 'tensor', scatter_dimension=0,...  166 us
    all_gather x2, waiting for transfers between devices, gather_rows(): return lax.all_gather(rows.astype(BF16), 'tensor', axis=0, tiled=True)  162 us
    pallas_call x1, Pallas kernels, gather_inputs(): pl.pallas_call(functools.partial(gather_body, n, cut), out_shape=(out(n,...  147 us
    unnamed x12, waiting for transfers between devices  123 us
    reduce_scatter x1, waiting for transfers between devices, shards(): lax.psum_scatter(mlp_partial, 'tensor', scatter_dimension=0, tiled=True)  75.7 us
    all_gather x1, blocking collectives, shards(): packed = lax.all_gather(packed, ('dp', 'tensor'), axis=0)  68.1 us
    dot_general x4, matrix products, dot_trans(): lax.dot_general(left, right, (((1,), (1,)), ((), ())), preferred_element_...  47.5 us
  transfers between devices with their start and end apart: 11, of which 11 were waited for; matrix products, arithmetic and copies ran while one was open for 7% of the time, Pallas kernels for 0%

profile of v1, /device:TPU:0, one launch (start us, length us, event | category | flops | bytes accessed | tf_op | source)
XLA Modules:
  0.0 1307.5 jit_solution(9028915237387373248)
XLA Ops:
  17.4 147.4 %gather_inputs.1 = (bf16[4,256,2048]{2,1,0:T(8,128)(2,1)S(1)}, bf16[4,256,2048]{2,1,0:T(8,128)(2,1)S(1)}, bf16[2048,1536]{1,0:T(8,128)(2,1)S(1)}, bf16[512,2048]...) custom-call(bf16[256,2048]{1,0:T(8,128)(2,1)S(1)} %copy-done, ...), custom_call_target="tpu_custom_call" | custom-call | tf_op jit(solution)/shard_map/gather_inputs/pallas_call | solution.py:226
  164.8 3.2 copy-done.10
  168.0 3.2 copy-done.11
  179.2 68.1 %all-gather.1 = f32[32,1,768]{2,1,0:T(1,128)S(1)} all-gather(f32[1,1,768]{2,1,0:T(1,128)S(1)} %reshape.392), channel_id=2, replica_groups=mesh['dp'=8,'tensor'=4] {'dp','tensor'}, dimensions={0}, use_global_device_ids=true | all-gather | bytes 101376 | tf_op jit(solution)/shard_map/all_gather | solution.py:374
  249.1 3.5 fusion.32
  252.6 6.9 add_convert_fusion
  265.5 29.3 %while.28 = (s32[]{:T(128)}, bf16[2,512,4,128]{3,1,2,0:T(8,128)(2,1)S(1)}, f32[2,4,512]{2,1,0:T(4,128)S(1)}, s32[2]{0:T(128)S(1)}, s32[]{:T(128)}, /*index=5*/bf...) while((s32[]{:T(128)}, ...), condition=%wide.region_5.6_spmd.clone, body=%wide.region_2.5_spmd.clone.sunk | while | flops 1111490048 | bytes 39396532 | solution.py:281
  268.1 4.0 fusion.112
  272.1 3.0 exponential_reduce_fusion.2
  275.2 4.9 fusion.113
  282.6 4.0 fusion.112
  286.7 3.0 exponential_reduce_fusion.2
  289.7 4.9 fusion.113
  296.6 4.3 convolution_convert_fusion.6
  301.2 72.9 %reduce-scatter.9.cloned.1.call-done = bf16[256,2048]{1,0:T(8,128)(2,1)} async-done(((bf16[1024,2048]{1,0:T(8,128)(2,1)}), bf16[256,2048]{1,0:T(8,128)(2,1)}) %reduce-scatter.9.cloned.1.call-update) | async-done | bytes 1048592 | tf_op jit(solution)/shard_map/reduce_scatter | solution.py:324
  379.7 81.1 %all-gather.5.cloned.1.call-done = bf16[1024,2048]{1,0:T(8,128)(2,1)} async-done(((bf16[256,2048]{1,0:T(8,128)(2,1)}), bf16[1024,2048]{1,0:T(8,128)(2,1)}) %all-gather.5.cloned.1.call-update) | async-done | bytes 4194320 | tf_op jit(solution)/shard_map/all_gather | solution.py:330
  460.8 14.7 %fusion.68 = f32[1024,2048]{1,0:T(8,128)} fusion(bf16[1024,2048]{1,0:T(8,128)(2,1)} %all-gather.5.cloned.1.call-done, bf16[2048,2048]{1,0:T(8,128)(2,1)} %copy-done.11), kind=kOutput, calls=%fused_computation.163 | convolution fusion | flops 8589934592 | bytes 20971520 | tf_op jit(solution)/shard_map/dot_general | solution.py:48
  475.5 19.6 %convert_reduce_fusion = (f32[2048]{0:T(1024)}, bf16[1024,2048]{1,0:T(8,128)(2,1)}) fusion(f32[1024,2048]{1,0:T(8,128)} %fusion.68, f32[2048]{0:T(1024)S(1)} %add.222, bf16[1024,2048]{1,0:T(8,128)(2,1)S(1)} %bitcast.176, bf16[2048,2048]{1,0:T(8,128)(2,1)} %copy-done.10), kind=kOutput, calls=%fused_computation.54 | convolution fusion | flops 8633972736 | bytes 25182208 | tf_op jit(solution)/shard_map/dot_general | solution.py:56
  495.1 12.0 convolution_convert_fusion.4
  507.2 16.5 %convolution_convert_fusion.5 = bf16[1024,2048]{1,0:T(8,128)(2,1)} fusion(bf16[2048,2048]{1,0:T(8,128)(2,1)} %copy-done.10, f32[1024,2048]{1,0:T(8,128)} %fusion.68, f32[2048]{0:T(1024)S(1)} %add.222), kind=kOutput, calls=%fused_computation.69 | convolution fusion | flops 8613003264 | bytes 20979712 | tf_op jit(solution)/shard_map/dot_general | solution.py:48
  524.5 58.1 %reduce-scatter.13.cloned.1.call-done = bf16[256,2048]{1,0:T(8,128)(2,1)} async-done(((bf16[1024,2048]{1,0:T(8,128)(2,1)}), bf16[256,2048]{1,0:T(8,128)(2,1)}) %reduce-scatter.13.cloned.1.call-update) | async-done | bytes 1048592 | tf_op jit(solution)/shard_map/reduce_scatter | solution.py:324
  582.6 3.7 fusion.52
  586.3 75.7 %reduce-scatter.11.cloned.1.call-done = bf16[256,2048]{1,0:T(8,128)(2,1)} async-done(((bf16[1024,2048]{1,0:T(8,128)(2,1)}), bf16[256,2048]{1,0:T(8,128)(2,1)}) %reduce-scatter.11.cloned.1.call-update) | async-done | bytes 1048592 | tf_op jit(solution)/shard_map/reduce_scatter | solution.py:416
  662.0 5.3 fusion.62
  669.8 81.4 %all-gather.7.cloned.1.call-done = bf16[1024,2048]{1,0:T(8,128)(2,1)} async-done(((bf16[256,2048]{1,0:T(8,128)(2,1)}), bf16[1024,2048]{1,0:T(8,128)(2,1)}) %all-gather.7.cloned.1.call-update) | async-done | bytes 4194320 | tf_op jit(solution)/shard_map/all_gather | solution.py:330
  751.2 4.5 convolution_convert_fusion.8
  758.3 57.1 %while.29 = (s32[]{:T(128)}, f32[1024,4,128]{0,2,1:T(8,128)}, f32[1024,4,128]{0,2,1:T(8,128)}, bf16[2,512,4,128]{3,1,2,0:T(8,128)(2,1)}, bf16[2,512,4,128]{3,1,2...) while((s32[]{:T(128)}, f32[1024,4,128]{0,2,1:T(8,128)}, ...), condition=%wide.region_17.18_spmd.clone, body=%wide.region_15.17_spmd.clone.sunk | while | flops 2712403456 | bytes 176211840 | solution.py:316
  764.6 5.1 multiply_reduce_fusion.4
  769.7 3.2 copy-done.17
  775.3 3.8 bitcast_add_fusion.4
  779.1 4.8 fusion.123
  792.3 5.1 multiply_reduce_fusion.4
  797.4 3.2 copy-done.17
  803.0 3.8 bitcast_add_fusion.4
  806.8 4.9 fusion.123
  811.7 3.7 bitcast_add_fusion.5
  822.7 11.3 convolution_convert_fusion.3
  834.2 14.0 %convolution_convert_fusion.1 = bf16[2048,2048]{1,0:T(8,128)(2,1)} fusion(bf16[1024,2048]{1,0:T(8,128)(2,1)} %all-gather.5.cloned.1.call-done, bf16[1024,2048]{1,0:T(8,128)(2,1)} %get-tuple-element.386), kind=kOutput, calls=%fused_computation.62 | convolution fusion | flops 8594128896 | bytes 16777216 | tf_op jit(solution)/shard_map/dot_general | solution.py:52
  848.9 15.9 %convolution_convert_fusion = bf16[2048,2048]{1,0:T(8,128)(2,1)} fusion(bf16[1024,2048]{1,0:T(8,128)(2,1)} %bitcast.175, f32[1024,2048]{1,0:T(8,128)} %fusion.68, f32[2048]{0:T(1024)S(1)} %copy-done.42), kind=kOutput, calls=%fused_computation.61 | convolution fusion | flops 8615100416 | bytes 20979712 | tf_op jit(solution)/shard_map/dot_general | solution.py:52
  866.0 5.9 convolution_convert_fusion.7
  874.5 35.1 %reduce-scatter.15.cloned.1.call-done = bf16[256,2048]{1,0:T(8,128)(2,1)} async-done(((bf16[1024,2048]{1,0:T(8,128)(2,1)}), bf16[256,2048]{1,0:T(8,128)(2,1)}) %reduce-scatter.15.cloned.1.call-update) | async-done | bytes 1048592 | tf_op jit(solution)/shard_map/reduce_scatter | solution.py:324
  913.0 11.4 convolution_convert_fusion.2
  924.4 60.4 %reduce-scatter.21.cloned.1.call-done = bf16[256,2048]{1,0:T(8,128)(2,1)} async-done(((bf16[2048,2048]{1,0:T(8,128)(2,1)}), bf16[256,2048]{1,0:T(8,128)(2,1)}) %reduce-scatter.21.cloned.1.call-update) | async-done | bytes 1048592 | tf_op jit(solution)/shard_map/reduce_scatter | solution.py:434
  987.6 72.4 %reduce-scatter.23.cloned.1.call-done = bf16[2048,256]{1,0:T(8,128)(2,1)} async-done(((bf16[2048,2048]{1,0:T(8,128)(2,1)}), bf16[2048,256]{1,0:T(8,128)(2,1)}) %reduce-scatter.23.cloned.1.call-update) | async-done | bytes 1048592 | tf_op jit(solution)/shard_map/reduce_scatter | solution.py:434
  1062.7 41.8 %reduce-scatter.19.cloned.1.call-done = bf16[512,256]{1,0:T(8,128)(2,1)} async-done(((bf16[512,2048]{1,0:T(8,128)(2,1)}), bf16[512,256]{1,0:T(8,128)(2,1)}) %reduce-scatter.19.cloned.1.call-update) | async-done | bytes 262160 | tf_op jit(solution)/shard_map/reduce_scatter | solution.py:434
  1106.3 3.3 fusion.44
  1109.6 122.4 %all-reduce.3.cloned.1.call-done = f32[32,768]{1,0:T(8,128)} async-done(((f32[32,768]{1,0:T(8,128)}), f32[32,768]{1,0:T(8,128)}) %all-reduce.3.cloned.1.call-update) | async-done | bytes 98320
  1236.3 62.1 %reduce-scatter.17.cloned.1.call-done = bf16[256,1536]{1,0:T(8,128)(2,1)} async-done(((bf16[2048,1536]{1,0:T(8,128)(2,1)}), bf16[256,1536]{1,0:T(8,128)(2,1)}) %reduce-scatter.17.cloned.1.call-update) | async-done | bytes 786448 | tf_op jit(solution)/shard_map/reduce_scatter | solution.py:434
  (285 shorter events, 91.9 us)
Async XLA Ops:
  7.2 367.0 %reduce-scatter.9.cloned.1.call-start = ((), (), s32[]{:S(2)}) async-start(), calls=%async_computation.8 | async-start | bytes 5242880 | tf_op jit(solution)/shard_map/reduce_scatter | solution.py:324
  175.3 3.6 copy-start.45
  175.3 3.6 copy-start.46
  175.3 3.7 copy-start.47
  175.3 3.7 copy-start.48
  175.3 3.7 copy-start.49
  175.3 3.7 copy-start.50
  175.3 3.7 copy-start.51
  175.3 3.7 copy-start.52
  176.0 76.6 %slice-start.2 = ((s8[6291456]{0:T(1024)(128)(4,1)}), s8[2097152]{0:T(1024)(128)(4,1)S(1)}, s32[]{:S(2)}) async-start(s8[6291456]{0:T(1024)(128)(4,1)} %bitcast.173), calls=%async_computation.21 | async-start | bytes 4194304
  248.2 4.4 copy-start.29
  252.6 6.9 copy-start.25
  265.5 31.1 %copy-start.16 = (bf16[512,2048]{1,0:T(8,128)(2,1)S(1)}, bf16[512,2048]{1,0:T(8,128)(2,1)}, u32[]{:S(2)}) copy-start(bf16[512,2048]{1,0:T(8,128)(2,1)} %copy-done.15) | copy-start | bytes 6291460
  300.9 73.2 %copy-start.1 = (bf16[256,2048]{1,0:T(8,128)(2,1)S(1)}, bf16[256,2048]{1,0:T(8,128)(2,1)}, u32[]{:S(2)}) copy-start(bf16[256,2048]{1,0:T(8,128)(2,1)} %hid.1) | copy-start | bytes 3145732
  301.0 159.9 %all-gather.5.cloned.1.call-start = ((), (), s32[]{:S(2)}) async-start(), calls=%async_computation.9 | async-start | bytes 5242880 | tf_op jit(solution)/shard_map/all_gather | solution.py:330
  379.4 203.2 %reduce-scatter.13.cloned.1.call-start = ((), (), s32[]{:S(2)}) async-start(), calls=%async_computation.11 | async-start | bytes 5242880 | tf_op jit(solution)/shard_map/reduce_scatter | solution.py:324
  379.7 127.5 %copy-start.41 = (f32[2048]{0:T(1024)}, f32[2048]{0:T(1024)S(1)}, u32[]{:S(2)}) copy-start(f32[2048]{0:T(1024)S(1)} %add.222) | copy-start | bytes 24580
  460.8 14.7 %copy-start.14 = (bf16[4,256,2048]{2,1,0:T(8,128)(2,1)S(1)}, bf16[4,256,2048]{2,1,0:T(8,128)(2,1)}, u32[]{:S(2)}) copy-start(bf16[4,256,2048]{2,1,0:T(8,128)(2,1)} %copy-done.13) | copy-start | bytes 12582916
  460.8 34.3 %slice-start = ((s8[8388608]{0:T(1024)(128)(4,1)}), s8[4194304]{0:T(1024)(128)(4,1)S(1)}, s32[]{:S(2)}) async-start(s8[8388608]{0:T(1024)(128)(4,1)} %bitcast.171), calls=%async_computation.19 | async-start | bytes 8388608
  475.5 19.6 %slice-start.1 = ((s8[8388608]{0:T(1024)(128)(4,1)}), s8[4194304]{0:T(1024)(128)(4,1)S(1)}, s32[]{:S(2)}) async-start(s8[8388608]{0:T(1024)(128)(4,1)} %bitcast.171), calls=%async_computation.20 | async-start | bytes 8388608
  507.1 154.9 %reduce-scatter.11.cloned.1.call-start = ((), (), s32[]{:S(2)}) async-start(), calls=%async_computation.10 | async-start | bytes 5242880 | tf_op jit(solution)/shard_map/reduce_scatter | solution.py:416
  523.7 138.4 %copy-start.39 = (f32[256]{0:T(256)S(1)}, f32[256]{0:T(256)}, u32[]{:S(2)}) copy-start(f32[256]{0:T(256)} %copy-done.38) | copy-start | bytes 3076
  523.7 227.5 %all-gather.7.cloned.1.call-start = ((), (), s32[]{:S(2)}) async-start(), calls=%async_computation.12 | async-start | bytes 5242880 | tf_op jit(solution)/shard_map/all_gather | solution.py:330
  586.3 81.0 %copy-start.36 = (f32[256]{0:T(256)}, f32[256]{0:T(256)S(1)}, u32[]{:S(2)}) copy-start(f32[256]{0:T(256)S(1)} %broadcast_multiply_fusion.4) | copy-start | bytes 3076
  669.8 239.8 %reduce-scatter.15.cloned.1.call-start = ((), (), s32[]{:S(2)}) async-start(), calls=%async_computation.13 | async-start | bytes 5242880 | tf_op jit(solution)/shard_map/reduce_scatter | solution.py:324
  775.3 8.7 slice-start.4
  775.3 3.8 copy-start.18
  775.3 8.6 slice-start.5
  779.1 7.0 copy-start.20
  803.0 8.7 slice-start.4
  803.0 3.8 copy-start.18
  803.0 8.7 slice-start.5
  806.8 8.6 copy-start.20
  822.7 11.4 copy-start.26
  834.1 150.7 %reduce-scatter.21.cloned.1.call-start = ((), (), s32[]{:S(2)}) async-start(), calls=%async_computation.16 | async-start | bytes 9437184 | tf_op jit(solution)/shard_map/reduce_scatter | solution.py:434
  848.2 211.8 %reduce-scatter.23.cloned.1.call-start = ((), (), s32[]{:S(2)}) async-start(), calls=%async_computation.17 | async-start | bytes 9437184 | tf_op jit(solution)/shard_map/reduce_scatter | solution.py:434
  864.8 7.3 copy-start.35
  864.8 7.4 copy-start.34
  864.8 7.5 copy-start.33
  864.9 7.6 copy-start.32
  864.9 7.6 copy-start.44
  864.9 239.6 %reduce-scatter.19.cloned.1.call-start = ((), (), s32[]{:S(2)}) async-start(), calls=%async_computation.15 | async-start | bytes 2359296 | tf_op jit(solution)/shard_map/reduce_scatter | solution.py:434
  872.0 37.6 %copy-start.2 = (bf16[256,2048]{1,0:T(8,128)(2,1)S(1)}, bf16[256,2048]{1,0:T(8,128)(2,1)}, u32[]{:S(2)}) copy-start(bf16[256,2048]{1,0:T(8,128)(2,1)} %hid.1) | copy-start | bytes 3145732
  872.0 37.6 %copy-start.30 = (f32[2048]{0:T(1024)S(1)}, f32[2048]{0:T(1024)}, u32[]{:S(2)}) copy-start(f32[2048]{0:T(1024)} %copy-done.29) | copy-start | bytes 24580
  872.0 37.6 %copy-start.37 = (f32[256]{0:T(256)S(1)}, f32[256]{0:T(256)}, u32[]{:S(2)}) copy-start(f32[256]{0:T(256)} %copy-done.36) | copy-start | bytes 3076
  872.0 360.0 %all-reduce.3.cloned.1.call-start = ((), (), s32[]{:S(2)}) async-start(), calls=%async_computation.18 | async-start | bytes 196608
  912.9 385.5 %reduce-scatter.17.cloned.1.call-start = ((), (), s32[]{:S(2)}) async-start(), calls=%async_computation.14 | async-start | bytes 7077888 | tf_op jit(solution)/shard_map/reduce_scatter | solution.py:434
  924.4 181.9 %copy-start.24 = (f32[256,2048]{1,0:T(8,128)S(1)}, f32[256,2048]{1,0:T(8,128)}, u32[]{:S(2)}) copy-start(f32[256,2048]{1,0:T(8,128)} %copy-done.23) | copy-start | bytes 6291460
  (28 other events, 55.5 us)
Sparse Core Ops, SparseCore 0:
  301.1 73.0 reduce-scatter.8
  379.5 81.2 all-gather.4
  507.2 75.2 reduce-scatter.12
  584.7 77.2 reduce-scatter.10
  669.9 81.2 all-gather.6
  834.2 75.2 reduce-scatter.14
  913.0 71.7 reduce-scatter.20
  988.7 71.2 reduce-scatter.22
  1063.3 41.1 reduce-scatter.18
  1111.4 120.5 all-reduce.2
  1235.8 62.5 reduce-scatter.16
